TPU v7x, 32 devices: a whole 2x2x4 slice. The times are simulated.
32 devices in a mesh: tile: 4 (over x, core), frame: 8 (over z, y).
Axes of the slice: x: 2, y: 2, z: 4, core: 2. Of those that a mesh axis runs over, the one named last changes fastest.
Arguments:
- queries: bfloat16 [8192, 1536], P(('tile', 'frame')), may hold values from -5 to 5
- keys: bfloat16 [8192, 1536], P(('tile', 'frame')), may hold values from -5 to 5
- values: bfloat16 [8192, 1536], P(('tile', 'frame')), may hold values from -6 to 6
- block_lists: int32 [64, 26], replicated, may hold values from -1 to 63, as said below
Outputs:
- attended: bfloat16 [8192, 1536], P(('tile', 'frame'))
Inputs may be any that keep to these rules, and one draw needn't show every extreme that they name: `block_lists`: block b belongs to spatial tile (b // 2) // 8 and frame group (b // 2) % 8. Row b lists first, without repeats, the key blocks that query block b attends to, then -1 to its end. Every listed block lies at a squared distance of at most 4 from block b in (tile, frame group), and all blocks of b's own tile and frame group are listed.
All inputs are finite; a program needn't handle non-finite values.
Results may differ from a plain program's by a relative error of at most 0.004.
Values may be sent and summed in bfloat16 or wider, within the bound.
A program may use at most 128 MiB of HBM per device.

v0:
```python
import functools
import math

import jax
import jax.numpy as jnp
from jax import lax
from jax.experimental import pallas as pl
from jax.experimental.pallas import tpu as pltpu
from jax.sharding import PartitionSpec as P

HEADS = 12
DH = 128
BLK = 128
CHUNKS = 3
PER = HEADS // CHUNKS
HALF = PER * DH
NEGATIVE = -1e30
SCALE = math.log2(math.e) / math.sqrt(DH)

SELF, PART, NEAR, ZA, ZB, X1, X2, X3, DIAG, PNEAR, PDIAG, XNEAR, XDIAG = range(13)
SLOTS = 13
GROUPS_OF_SLOTS = (
    (SELF,),
    (PART,),
    (NEAR, ZA, ZB, X1, X2, X3),
    (DIAG, PNEAR, XNEAR),
    (PDIAG, XDIAG),
)


def geometry():
    tiles, groups = lax.axis_size("tile"), lax.axis_size("frame")
    t, g = lax.axis_index("tile"), lax.axis_index("frame")
    f = 2 * lax.rem(t, 2) - 1
    d = 2 * lax.rem(g, 2) - 1
    offsets = (
        (0, 0), (-f, 0), (0, -d), (0, 2 * d), (0, -2 * d), (f, 0), (2 * f, 0), (-2 * f, 0),
        (0, d), (-f, -d), (-f, d), (f, -d), (f, d),
    )
    return tiles, groups, t, g, f, d, offsets


def kernel(q_ref, k_ref, v_ref, bias_ref, o_ref, buf, acc, top, total, own_sem, send_sem, recv_sem):
    tiles, groups, t, g, f, d, offsets = geometry()

    def inside(dt, dg):
        a, b = t + dt, g + dg
        return (a >= 0) & (a < tiles) & (b >= 0) & (b < groups)

    valid = [inside(*offset) for offset in offsets]
    peers = ((-f, 0), (0, -d), (0, 2), (0, -2), (f, 0), (2, 0), (-2, 0))

    def own_copy(j, which):
        ref = (k_ref, v_ref)[which]
        return pltpu.make_async_copy(
            ref.at[:, pl.ds(j * HALF, HALF)],
            buf.at[SELF, j, :, pl.ds(which * HALF, HALF)],
            own_sem.at[j, which],
        )

    for j in range(CHUNKS):
        for which in range(2):
            own_copy(j, which).start()

    barrier = pltpu.get_barrier_semaphore()
    for dt, dg in peers:
        @pl.when(inside(dt, dg))
        def _():
            pl.semaphore_signal(
                barrier, inc=1, device_id=(t + dt, g + dg), device_id_type=pl.DeviceIdType.MESH
            )
    pl.semaphore_wait(barrier, sum(inside(*peer).astype(jnp.int32) for peer in peers))

    every = (0, 1, 2)
    moves = (
        (SELF, NEAR, (0, -d), True, every),
        (SELF, ZA, (0, -2 * d), True, every),
        (SELF, ZB, (0, 2 * d), True, every),
        (SELF, X1, (f, 0), True, every),
        (SELF, X2, (-2 * f, 0), True, every),
        (SELF, PART, (-f, 0), True, every),
        (NEAR, DIAG, (0, -2 * d), True, (0, 1)),
        (ZB, DIAG, (0, -d), True, (2,)),
        (NEAR, XNEAR, (f, 0), True, (2,)),
        (X1, XNEAR, (0, -d), True, (0, 1)),
        (NEAR, PNEAR, (-f, 0), True, every),
        (X1, X3, (-f, 0), True, every),
        (DIAG, XDIAG, (f, 0), True, every),
        (DIAG, PDIAG, (-f, 0), True, every),
    )

    def among(j, chunks):
        hit = j == chunks[0]
        for other in chunks[1:]:
            hit = hit | (j == other)
        return hit

    def each_move(j, sources, act):
        for index, (source, slot, place, _, chunks) in enumerate(moves):
            if source not in sources:
                continue
            where = inside(*place) & valid[source]
            if len(chunks) < CHUNKS:
                where = where & among(j, chunks)

            @pl.when(where)
            def _():
                act(
                    pltpu.make_async_remote_copy(
                        src_ref=buf.at[source, j],
                        dst_ref=buf.at[slot, j],
                        send_sem=send_sem.at[index, j],
                        recv_sem=recv_sem.at[slot, j],
                        device_id=(t + place[0], g + place[1]),
                        device_id_type=pl.DeviceIdType.MESH,
                    )
                )

    def arrived(slot, j):
        pltpu.make_async_copy(buf.at[slot, j], buf.at[slot, j], recv_sem.at[slot, j]).wait()

    lane = lax.broadcasted_iota(jnp.int32, (1, 2 * BLK), 1)

    def compute(slot, j):
        upper = jnp.where(lane < BLK, bias_ref[4 * slot], bias_ref[4 * slot + 1])
        lower = jnp.where(lane < BLK, bias_ref[4 * slot + 2], bias_ref[4 * slot + 3])
        for hh in range(PER):
            head = j * PER + hh
            cols = pl.ds(pl.multiple_of(head * DH, DH), DH)
            k = buf[slot, j, :, hh * DH:(hh + 1) * DH]
            v = buf[slot, j, :, HALF + hh * DH:HALF + (hh + 1) * DH]
            s = lax.dot_general(
                q_ref[:, cols], k, (((1,), (1,)), ((), ())), preferred_element_type=jnp.float32
            )
            s = jnp.concatenate([s[:BLK] * SCALE + upper, s[BLK:] * SCALE + lower], axis=0)
            peak = jnp.max(s, axis=1, keepdims=True)
            if slot == SELF:
                new = jnp.broadcast_to(peak, (2 * BLK, DH))
            else:
                old = top[head]
                new = jnp.maximum(old, peak)
            p = jnp.exp2(s - jnp.concatenate([new, new], axis=1))
            part = p[:, :DH] + p[:, DH:]
            mixed = jnp.dot(p.astype(jnp.bfloat16), v, preferred_element_type=jnp.float32)
            if slot != SELF:
                rescale = jnp.exp2(old - new)
                part = part + total[head] * rescale
                mixed = mixed + acc[:, cols] * rescale
            top[head] = new
            total[head] = part
            acc[:, cols] = mixed

    for j in range(CHUNKS):
        own_copy(j, 0).wait()
        own_copy(j, 1).wait()
        each_move(j, (SELF,), lambda copy: copy.start())

    for members in GROUPS_OF_SLOTS:
        def step(j, carry):
            if members != (SELF,):
                for slot in members:
                    @pl.when(valid[slot])
                    def _():
                        arrived(slot, j)
                    each_move(j, (slot,), lambda copy: copy.start())
            for slot in members:
                @pl.when(valid[slot])
                def _():
                    compute(slot, j)
            return carry
        lax.fori_loop(0, CHUNKS, step, 0)

    for head in range(HEADS):
        denom = jnp.sum(total[head], axis=1, keepdims=True)
        cols = slice(head * DH, (head + 1) * DH)
        o_ref[:, cols] = (acc[:, cols] / denom).astype(jnp.bfloat16)

    def drain(j, carry):
        each_move(j, tuple(range(SLOTS)), lambda copy: copy.wait_send())
        return carry
    lax.fori_loop(0, CHUNKS, drain, 0)


def shards(queries, keys, values, block_lists):
    tiles, groups, t, g, f, d, offsets = geometry()
    rows, width = queries.shape
    nblocks = rows // BLK
    start = (t * groups + g) * nblocks
    own = lax.dynamic_slice(block_lists, (start, jnp.int32(0)), (nblocks, block_lists.shape[1]))
    first = jnp.stack([((t + dt) * groups + g + dg) * nblocks for dt, dg in offsets])
    ids = first[:, None, None] + jnp.arange(nblocks, dtype=jnp.int32)[None, None, :]
    hit = jnp.any(own[None, :, None, :] == ids[..., None], axis=3)
    bias = jnp.where(hit, 0.0, NEGATIVE).astype(jnp.float32).reshape(-1)
    vmem = pl.BlockSpec(memory_space=pltpu.VMEM)
    return pl.pallas_call(
        kernel,
        out_shape=jax.ShapeDtypeStruct((rows, width), jnp.bfloat16),
        in_specs=[
            vmem,
            pl.BlockSpec(memory_space=pl.ANY),
            pl.BlockSpec(memory_space=pl.ANY),
            pl.BlockSpec(memory_space=pltpu.SMEM),
        ],
        out_specs=vmem,
        scratch_shapes=[
            pltpu.VMEM((SLOTS, CHUNKS, rows, 2 * HALF), jnp.bfloat16),
            pltpu.VMEM((rows, width), jnp.float32),
            pltpu.VMEM((HEADS, rows, DH), jnp.float32),
            pltpu.VMEM((HEADS, rows, DH), jnp.float32),
            pltpu.SemaphoreType.DMA((CHUNKS, 2)),
            pltpu.SemaphoreType.DMA((14, CHUNKS)),
            pltpu.SemaphoreType.DMA((SLOTS, CHUNKS)),
        ],
        compiler_params=pltpu.CompilerParams(
            collective_id=0, has_side_effects=True, vmem_limit_bytes=48 * 1024 * 1024
        ),
    )(queries, keys, values, bias)


def solution(mesh):
    placed = P(("tile", "frame"), None)
    return jax.shard_map(
        shards, mesh=mesh, in_specs=(placed, placed, placed, P()), out_specs=placed, check_vma=False
    )
```

profile of v0, /device:TPU:5, one launch (start us, length us, event | category | flops | bytes accessed | tf_op | source)
XLA Modules:
  0.0 83.4 jit_solution(9212662427842465497)
XLA Ops:
  0.0 0.0 copy-start
  0.0 0.1 stack.55
  0.1 0.6 copy-done
  0.7 0.1 constant_dynamic-slice_fusion
  0.8 0.1 copy.7
  0.9 0.2 compare_reduce_fusion
  1.1 0.1 copy.8
  1.2 0.1 select_n.13.bias_ref
  1.3 0.0 copy-start.1
  1.3 1.1 %copy-done.1 = bf16[256,1536]{1,0:T(8,128)(2,1)S(1)} copy-done((bf16[256,1536]{1,0:T(8,128)(2,1)S(1)}, bf16[256,1536]{1,0:T(8,128)(2,1)}, u32[]{:S(2)}) %copy-start.1) | copy-done | bytes 786456
  2.5 0.0 copy-start.2
  2.5 1.1 %copy-done.2 = bf16[256,1536]{1,0:T(8,128)(2,1)S(1)} copy-done((bf16[256,1536]{1,0:T(8,128)(2,1)S(1)}, bf16[256,1536]{1,0:T(8,128)(2,1)}, u32[]{:S(2)}) %copy-start.2) | copy-done | bytes 786456
  3.6 0.0 copy-start.3
  3.6 1.1 %copy-done.3 = bf16[256,1536]{1,0:T(8,128)(2,1)S(1)} copy-done((bf16[256,1536]{1,0:T(8,128)(2,1)S(1)}, bf16[256,1536]{1,0:T(8,128)(2,1)}, u32[]{:S(2)}) %copy-start.3) | copy-done | bytes 786456
  4.7 77.8 %shard_map.46 = bf16[256,1536]{1,0:T(8,128)(2,1)S(1)} custom-call(bf16[256,1536]{1,0:T(8,128)(2,1)S(1)} %copy-done.1, bf16[256,1536]{1,0:T(8,128)(2,1)S(1)} %copy-done.2, bf16[256,1536]{1,0:T(8,128)(2,1)S(1)} %copy-done.3, f32[52]{0:T(128)S(1)} %select_n.13.bias_ref), custom_call_target="tpu_custom_call" | custom-call | tf_op jit(solution)/shard_map/pallas_call | solution.py:195
  82.5 0.9 %copy.10 = bf16[256,1536]{1,0:T(8,128)(2,1)} copy(bf16[256,1536]{1,0:T(8,128)(2,1)S(1)} %shard_map.46) | data formatting | bytes 1572864
  (2 shorter events, 0.0 us)
Async XLA Ops:
  0.0 0.7 copy-start
  1.3 1.1 %copy-start.1 = (bf16[256,1536]{1,0:T(8,128)(2,1)S(1)}, bf16[256,1536]{1,0:T(8,128)(2,1)}, u32[]{:S(2)}) copy-start(bf16[256,1536]{1,0:T(8,128)(2,1)} %q_ref.1) | copy-start | bytes 2359300
  2.5 1.1 %copy-start.2 = (bf16[256,1536]{1,0:T(8,128)(2,1)S(1)}, bf16[256,1536]{1,0:T(8,128)(2,1)}, u32[]{:S(2)}) copy-start(bf16[256,1536]{1,0:T(8,128)(2,1)} %k_ref.1) | copy-start | bytes 2359300
  3.6 1.1 %copy-start.3 = (bf16[256,1536]{1,0:T(8,128)(2,1)S(1)}, bf16[256,1536]{1,0:T(8,128)(2,1)}, u32[]{:S(2)}) copy-start(bf16[256,1536]{1,0:T(8,128)(2,1)} %v_ref.1) | copy-start | bytes 2359300
where the time goes:
time: 83.7 us; the launch traced here: 83.4 us
  Pallas kernels  77.8 us (93%)
  local copies, waits for them, and re-layouts  5.36 us (6%)
    pallas_call x1, Pallas kernels, shards(): pl.pallas_call(kernel, out_shape=jax.ShapeDtypeStruct((rows, width), jnp....  77.8 us
    unnamed x9, local copies, waits for them, and re-layouts  4.9 us

commit v1 on v0

--- a/solution.py
+++ b/solution.py
@@ -19,13 +19,15 @@
 
 SELF, PART, NEAR, ZA, ZB, X1, X2, X3, DIAG, PNEAR, PDIAG, XNEAR, XDIAG = range(13)
 SLOTS = 13
-GROUPS_OF_SLOTS = (
-    (SELF,),
-    (PART,),
-    (NEAR, ZA, ZB, X1, X2, X3),
-    (DIAG, PNEAR, XNEAR),
-    (PDIAG, XDIAG),
+STAGES = (
+    (0, (SELF,)),
+    (1, (PART, NEAR, ZA, ZB, X1, X2)),
+    (2, (DIAG, X3, PNEAR, XNEAR)),
+    (3, (PDIAG, XDIAG)),
 )
+RELAYED = (NEAR, ZB, X1, DIAG)
+DIAG_Z, DIAG_Y = (0,), (1, 2)
+XNEAR_X, XNEAR_Y = (0, 1), (2,)
 
 
 def geometry():
@@ -40,7 +42,7 @@
     return tiles, groups, t, g, f, d, offsets
 
 
-def kernel(q_ref, k_ref, v_ref, bias_ref, o_ref, buf, acc, top, total, own_sem, send_sem, recv_sem):
+def kernel(q_hbm, k_ref, v_ref, lists_ref, o_ref, q_ref, bias, buf, acc, top, total, q_sem, own_sem, send_sem, recv_sem):
     tiles, groups, t, g, f, d, offsets = geometry()
 
     def inside(dt, dg):
@@ -61,6 +63,8 @@
     for j in range(CHUNKS):
         for which in range(2):
             own_copy(j, which).start()
+    q_copy = pltpu.make_async_copy(q_hbm, q_ref, q_sem)
+    q_copy.start()
 
     barrier = pltpu.get_barrier_semaphore()
     for dt, dg in peers:
@@ -71,22 +75,22 @@
             )
     pl.semaphore_wait(barrier, sum(inside(*peer).astype(jnp.int32) for peer in peers))
 
-    every = (0, 1, 2)
+    every = tuple(range(CHUNKS))
     moves = (
-        (SELF, NEAR, (0, -d), True, every),
-        (SELF, ZA, (0, -2 * d), True, every),
-        (SELF, ZB, (0, 2 * d), True, every),
-        (SELF, X1, (f, 0), True, every),
-        (SELF, X2, (-2 * f, 0), True, every),
-        (SELF, PART, (-f, 0), True, every),
-        (NEAR, DIAG, (0, -2 * d), True, (0, 1)),
-        (ZB, DIAG, (0, -d), True, (2,)),
-        (NEAR, XNEAR, (f, 0), True, (2,)),
-        (X1, XNEAR, (0, -d), True, (0, 1)),
-        (NEAR, PNEAR, (-f, 0), True, every),
-        (X1, X3, (-f, 0), True, every),
-        (DIAG, XDIAG, (f, 0), True, every),
-        (DIAG, PDIAG, (-f, 0), True, every),
+        (SELF, NEAR, (0, -d), every),
+        (SELF, ZA, (0, -2 * d), every),
+        (SELF, ZB, (0, 2 * d), every),
+        (SELF, X1, (f, 0), every),
+        (SELF, X2, (-2 * f, 0), every),
+        (SELF, PART, (-f, 0), every),
+        (NEAR, DIAG, (0, -2 * d), DIAG_Z),
+        (ZB, DIAG, (0, -d), DIAG_Y),
+        (NEAR, XNEAR, (f, 0), XNEAR_X),
+        (X1, XNEAR, (0, -d), XNEAR_Y),
+        (NEAR, PNEAR, (-f, 0), every),
+        (X1, X3, (-f, 0), every),
+        (DIAG, XDIAG, (f, 0), every),
+        (DIAG, PDIAG, (-f, 0), every),
     )
 
     def among(j, chunks):
@@ -96,7 +100,7 @@
         return hit
 
     def each_move(j, sources, act):
-        for index, (source, slot, place, _, chunks) in enumerate(moves):
+        for index, (source, slot, place, chunks) in enumerate(moves):
             if source not in sources:
                 continue
             where = inside(*place) & valid[source]
@@ -119,11 +123,28 @@
     def arrived(slot, j):
         pltpu.make_async_copy(buf.at[slot, j], buf.at[slot, j], recv_sem.at[slot, j]).wait()
 
-    lane = lax.broadcasted_iota(jnp.int32, (1, 2 * BLK), 1)
+    def finish(j):
+        for hh in range(PER):
+            head = j * PER + hh
+            cols = pl.ds(pl.multiple_of(head * DH, DH), DH)
+            denom = jnp.sum(total[head], axis=1, keepdims=True)
+            o_ref[:, cols] = (acc[:, cols] / denom).astype(jnp.bfloat16)
+
+    def mask_rows():
+        lists = lists_ref[...]
+        block = lax.broadcasted_iota(jnp.int32, lists.shape, 1)
+        second = lax.broadcasted_iota(jnp.int32, (1, 2 * BLK), 1) // BLK
+        for half in range(2):
+            mine = 2 * (t * groups + g) + half
+            listed = jnp.sum(jnp.where(block == mine, lists, 0), axis=1, keepdims=True)
+            for slot, (dt, dg) in enumerate(offsets):
+                ids = 2 * ((t + dt) * groups + g + dg) + second
+                hit = jnp.max(jnp.where(listed == ids, 1, 0), axis=0, keepdims=True)
+                bias[2 * slot + half:2 * slot + half + 1, :] = jnp.where(hit > 0, 0.0, NEGATIVE)
 
     def compute(slot, j):
-        upper = jnp.where(lane < BLK, bias_ref[4 * slot], bias_ref[4 * slot + 1])
-        lower = jnp.where(lane < BLK, bias_ref[4 * slot + 2], bias_ref[4 * slot + 3])
+        upper = bias[2 * slot:2 * slot + 1, :]
+        lower = bias[2 * slot + 1:2 * slot + 2, :]
         for hh in range(PER):
             head = j * PER + hh
             cols = pl.ds(pl.multiple_of(head * DH, DH), DH)
@@ -150,30 +171,44 @@
             total[head] = part
             acc[:, cols] = mixed
 
-    for j in range(CHUNKS):
-        own_copy(j, 0).wait()
-        own_copy(j, 1).wait()
-        each_move(j, (SELF,), lambda copy: copy.start())
-
-    for members in GROUPS_OF_SLOTS:
-        def step(j, carry):
-            if members != (SELF,):
+    def step(tick, carry):
+        @pl.when(tick < CHUNKS)
+        def _():
+            own_copy(tick, 0).wait()
+            own_copy(tick, 1).wait()
+            each_move(tick, (SELF,), lambda copy: copy.start())
+
+        @pl.when(tick == 0)
+        def _():
+            mask_rows()
+            q_copy.wait()
+
+        for lag, members in STAGES:
+            j = tick - lag
+
+            @pl.when((j >= 0) & (j < CHUNKS))
+            def _():
+                for slot in members:
+                    if slot in RELAYED:
+                        @pl.when(valid[slot])
+                        def _():
+                            arrived(slot, j)
+                        each_move(j, (slot,), lambda copy: copy.start())
+        for lag, members in STAGES:
+            j = tick - lag
+
+            @pl.when((j >= 0) & (j < CHUNKS))
+            def _():
                 for slot in members:
                     @pl.when(valid[slot])
                     def _():
-                        arrived(slot, j)
-                    each_move(j, (slot,), lambda copy: copy.start())
-            for slot in members:
-                @pl.when(valid[slot])
-                def _():
-                    compute(slot, j)
-            return carry
-        lax.fori_loop(0, CHUNKS, step, 0)
-
-    for head in range(HEADS):
-        denom = jnp.sum(total[head], axis=1, keepdims=True)
-        cols = slice(head * DH, (head + 1) * DH)
-        o_ref[:, cols] = (acc[:, cols] / denom).astype(jnp.bfloat16)
+                        if slot != SELF and slot not in RELAYED:
+                            arrived(slot, j)
+                        compute(slot, j)
+                if members == STAGES[-1][1]:
+                    finish(j)
+        return carry
+    lax.fori_loop(0, CHUNKS + STAGES[-1][0], step, 0)
 
     def drain(j, carry):
         each_move(j, tuple(range(SLOTS)), lambda copy: copy.wait_send())
@@ -182,39 +217,34 @@
 
 
 def shards(queries, keys, values, block_lists):
-    tiles, groups, t, g, f, d, offsets = geometry()
     rows, width = queries.shape
-    nblocks = rows // BLK
-    start = (t * groups + g) * nblocks
-    own = lax.dynamic_slice(block_lists, (start, jnp.int32(0)), (nblocks, block_lists.shape[1]))
-    first = jnp.stack([((t + dt) * groups + g + dg) * nblocks for dt, dg in offsets])
-    ids = first[:, None, None] + jnp.arange(nblocks, dtype=jnp.int32)[None, None, :]
-    hit = jnp.any(own[None, :, None, :] == ids[..., None], axis=3)
-    bias = jnp.where(hit, 0.0, NEGATIVE).astype(jnp.float32).reshape(-1)
     vmem = pl.BlockSpec(memory_space=pltpu.VMEM)
     return pl.pallas_call(
         kernel,
         out_shape=jax.ShapeDtypeStruct((rows, width), jnp.bfloat16),
         in_specs=[
-            vmem,
             pl.BlockSpec(memory_space=pl.ANY),
             pl.BlockSpec(memory_space=pl.ANY),
-            pl.BlockSpec(memory_space=pltpu.SMEM),
+            pl.BlockSpec(memory_space=pl.ANY),
+            vmem,
         ],
         out_specs=vmem,
         scratch_shapes=[
+            pltpu.VMEM((rows, width), jnp.bfloat16),
+            pltpu.VMEM((2 * SLOTS, rows), jnp.float32),
             pltpu.VMEM((SLOTS, CHUNKS, rows, 2 * HALF), jnp.bfloat16),
             pltpu.VMEM((rows, width), jnp.float32),
             pltpu.VMEM((HEADS, rows, DH), jnp.float32),
             pltpu.VMEM((HEADS, rows, DH), jnp.float32),
+            pltpu.SemaphoreType.DMA,
             pltpu.SemaphoreType.DMA((CHUNKS, 2)),
             pltpu.SemaphoreType.DMA((14, CHUNKS)),
             pltpu.SemaphoreType.DMA((SLOTS, CHUNKS)),
         ],
         compiler_params=pltpu.CompilerParams(
-            collective_id=0, has_side_effects=True, vmem_limit_bytes=48 * 1024 * 1024
+            collective_id=0, has_side_effects=True, vmem_limit_bytes=67043328
         ),
-    )(queries, keys, values, bias)
+    )(queries, keys, values, block_lists.T)
 
 
 def solution(mesh):

time: 83.7 us -> 75.4 us (0.901); the launches traced: 83.4 us -> 74.1 us
  Pallas kernels: 77.8 us -> 72 us
  local copies, waits for them, and re-layouts: 5.36 us -> 2.06 us
    pallas_call x1, Pallas kernels: 77.8 us -> 72 us  [shards(): pl.pallas_call(kernel, out_shape=jax.ShapeDtypeStruct((rows, width), jnp....]
    unnamed x9 -> x1, local copies, waits for them, and re-layouts: 4.9 us -> 2.06 us
where the time goes in v1:
time: 75.4 us; the launch traced here: 74.1 us
  Pallas kernels  72 us (95%)
  local copies, waits for them, and re-layouts  2.06 us (3%)
    pallas_call x1, Pallas kernels, shards(): pl.pallas_call(kernel, out_shape=jax.ShapeDtypeStruct((rows, width), jnp....  72 us
    unnamed x1, local copies, waits for them, and re-layouts  2.06 us

profile of v1, /device:TPU:5, one launch (start us, length us, event | category | flops | bytes accessed | tf_op | source)
XLA Modules:
  0.0 74.1 jit_solution(5285921935980666528)
XLA Ops:
  0.0 72.0 %shard_map.46 = bf16[256,1536]{1,0:T(8,128)(2,1)} custom-call(bf16[256,1536]{1,0:T(8,128)(2,1)} %q_hbm.1, bf16[256,1536]{1,0:T(8,128)(2,1)} %k_ref.1, bf16[256,1536]{1,0:T(8,128)(2,1)} %v_ref.1, s32[26,64]{1,0:T(8,128)} %bitcast.1), custom_call_target="tpu_custom_call" | custom-call | tf_op jit(solution)/shard_map/pallas_call | solution.py:222
  72.1 2.1 %copy.6 = bf16[256,1536]{1,0:T(8,128)(2,1)} copy(bf16[256,1536]{1,0:T(8,128)(2,1)} %shard_map.46) | data formatting | bytes 1572864
